TPU v7x, 32 devices: a whole 2x2x4 slice. The times are simulated.
32 devices in a mesh: dp: 2 (over core), ctx: 16 (over z, y, x).
Axes of the slice: x: 2, y: 2, z: 4, core: 2. Of those that a mesh axis runs over, the one named last changes fastest.
Arguments:
- layer_in: bfloat16 [2, 4096, 768], P('dp', 'ctx'), may hold values from -6 to 6
- out_grad: bfloat16 [2, 4096, 768], P('dp', 'ctx'), may hold values from -6 to 6
- first_gain: bfloat16 [768], P('dp'), may hold values from 0.099609375 to 1.8984375
- query_weight: bfloat16 [768, 768], P('dp'), may hold values from -0.21875 to 0.21875
- key_weight: bfloat16 [768, 768], P('dp'), may hold values from -0.21875 to 0.21875
- value_weight: bfloat16 [768, 768], P('dp'), may hold values from -0.21875 to 0.21875
- output_weight: bfloat16 [768, 768], P('dp'), may hold values from -6 to 6
- second_gain: bfloat16 [768], P('dp'), may hold values from 0.099609375 to 1.8984375
- gate_weight: bfloat16 [768, 2048], P('dp'), may hold values from -0.21875 to 0.21875
- up_weight: bfloat16 [768, 2048], P('dp'), may hold values from -0.21875 to 0.21875
- down_weight: bfloat16 [2048, 768], P('dp'), may hold values from -0.125 to 0.125
Outputs:
- layer_out: bfloat16 [2, 4096, 768], P('dp', 'ctx')
- in_grad: bfloat16 [2, 4096, 768], P('dp', 'ctx')
- first_gain_grad: float32 [768], P('dp')
- query_grad: float32 [768, 768], P('dp')
- key_grad: float32 [768, 768], P('dp')
- value_grad: float32 [768, 768], P('dp')
- output_grad: float32 [768, 768], P('dp')
- second_gain_grad: float32 [768], P('dp')
- gate_grad: float32 [768, 2048], P('dp')
- up_grad: float32 [768, 2048], P('dp')
- down_grad: float32 [2048, 768], P('dp')
All inputs are finite; a program needn't handle non-finite values.
Results may differ from a plain program's by a relative error of at most 0.02.
Values may be sent and summed in bfloat16 or wider, within the bound.
No kernel may reach another device: no remote copies, remote signals or barrier semaphores. Data moves between devices by JAX's collectives and lax.ppermute only.
A program may use at most 448 MiB of HBM per device.

v0:
```python
import jax
import jax.numpy as jnp
from jax import lax
from jax.sharding import PartitionSpec as P

HEADS = 12
HEAD_DIM = 64
EPS = 1e-06


def normed(rows, gain):
    return rows * lax.rsqrt(jnp.mean(rows * rows, axis=-1, keepdims=True) + EPS) * gain


def gated(gate, upper):
    return jax.nn.gelu(gate, approximate=True) * upper


def heads_of(rows):
    return rows.reshape(rows.shape[0], HEADS, HEAD_DIM)


def scores_of(query, keys):
    return jnp.einsum(
        "qhd,khd->hqk", heads_of(query), heads_of(keys), preferred_element_type=jnp.float32
    ) * HEAD_DIM ** (-0.5)


def attend(operands):
    query, keys, values = operands
    scores = scores_of(query, keys)
    top = jnp.max(scores, axis=-1, keepdims=True)
    expd = jnp.exp(scores - top)
    total = jnp.sum(expd, axis=-1, keepdims=True)
    probs = (expd / total).astype(jnp.bfloat16)
    mixed = jnp.einsum("hqk,khd->qhd", probs, heads_of(values), preferred_element_type=jnp.float32)
    mixed = mixed.reshape(query.shape[0], HEADS * HEAD_DIM).astype(jnp.bfloat16)
    return (mixed, (top + jnp.log(total))[..., 0])


def back_core(query, keys, values, grad_mix, logsum):
    probs = jnp.exp(scores_of(query, keys) - logsum[..., None])
    grad_prob = jnp.einsum(
        "qhd,khd->hqk", heads_of(grad_mix), heads_of(values), preferred_element_type=jnp.float32
    )
    delta = jnp.sum(grad_prob * probs, axis=-1)
    grad_score = (probs * (grad_prob - delta[..., None])).astype(jnp.bfloat16)
    return (probs, grad_score, delta)


def query_part(grad_score, keys, count):
    grad_query = jnp.einsum(
        "hqk,khd->qhd", grad_score, heads_of(keys), preferred_element_type=jnp.float32
    ) * HEAD_DIM ** (-0.5)
    return grad_query.reshape(count, HEADS * HEAD_DIM).astype(jnp.bfloat16)


def attend_back(operands):
    query, keys, values, grad_mix, logsum = operands
    probs, grad_score, delta = back_core(query, keys, values, grad_mix, logsum)
    grad_query = query_part(grad_score, keys, query.shape[0])
    grad_keys = jnp.einsum(
        "hqk,qhd->khd", grad_score, heads_of(query), preferred_element_type=jnp.float32
    ) * HEAD_DIM ** (-0.5)
    grad_values = jnp.einsum(
        "hqk,qhd->khd",
        probs.astype(jnp.bfloat16),
        heads_of(grad_mix),
        preferred_element_type=jnp.float32,
    )
    return (
        grad_query,
        grad_keys.reshape(keys.shape[0], -1),
        grad_values.reshape(keys.shape[0], -1),
    )


def product(left, right):
    return jnp.dot(left, right, preferred_element_type=jnp.float32)


def on_device(
    layer_in,
    out_grad,
    first_gain,
    query_weight,
    key_weight,
    value_weight,
    output_weight,
    second_gain,
    gate_weight,
    up_weight,
    down_weight,
):
    seqs, local, width = layer_in.shape
    rows = seqs * local

    def shaped(matrix):
        return matrix.reshape(seqs, local, width)

    gain_one, w_query, w_key, w_value, w_output = (
        lax.all_gather(first_gain, "dp", axis=0, tiled=True),
        lax.all_gather(query_weight, "dp", axis=0, tiled=True),
        lax.all_gather(key_weight, "dp", axis=0, tiled=True),
        lax.all_gather(value_weight, "dp", axis=0, tiled=True),
        lax.all_gather(output_weight, "dp", axis=0, tiled=True),
    )
    inputs = layer_in.reshape(rows, width).astype(jnp.float32)
    gain_one_f = gain_one.astype(jnp.float32)
    normal_one = normed(inputs, gain_one_f).astype(jnp.bfloat16)
    query = product(normal_one, w_query).astype(jnp.bfloat16)
    keys = product(normal_one, w_key).astype(jnp.bfloat16)
    values = product(normal_one, w_value).astype(jnp.bfloat16)
    keys_all, values_all = (
        lax.all_gather(shaped(keys), "ctx", axis=1, tiled=True),
        lax.all_gather(shaped(values), "ctx", axis=1, tiled=True),
    )
    mixed, logsum = lax.map(attend, (shaped(query), keys_all, values_all))
    mixed_rows = mixed.reshape(rows, width)
    middle = inputs + product(mixed_rows, w_output)
    gain_two, w_gate, w_up, w_down = (
        lax.all_gather(second_gain, "dp", axis=0, tiled=True),
        lax.all_gather(gate_weight, "dp", axis=0, tiled=True),
        lax.all_gather(up_weight, "dp", axis=0, tiled=True),
        lax.all_gather(down_weight, "dp", axis=0, tiled=True),
    )
    gain_two_f = gain_two.astype(jnp.float32)
    normal_two = normed(middle, gain_two_f).astype(jnp.bfloat16)
    gate = product(normal_two, w_gate)
    upper = product(normal_two, w_up)
    hidden = gated(gate, upper).astype(jnp.bfloat16)
    result = middle + product(hidden, w_down)
    layer_out = result.astype(jnp.bfloat16).reshape(seqs, local, width)
    gain_one, w_query, w_key, w_value, w_output = (
        lax.all_gather(first_gain, "dp", axis=0, tiled=True),
        lax.all_gather(query_weight, "dp", axis=0, tiled=True),
        lax.all_gather(key_weight, "dp", axis=0, tiled=True),
        lax.all_gather(value_weight, "dp", axis=0, tiled=True),
        lax.all_gather(output_weight, "dp", axis=0, tiled=True),
    )
    gain_two, w_gate, w_up, w_down = (
        lax.all_gather(second_gain, "dp", axis=0, tiled=True),
        lax.all_gather(gate_weight, "dp", axis=0, tiled=True),
        lax.all_gather(up_weight, "dp", axis=0, tiled=True),
        lax.all_gather(down_weight, "dp", axis=0, tiled=True),
    )
    gain_one_f = gain_one.astype(jnp.float32)
    gain_two_f = gain_two.astype(jnp.float32)
    grad_rows = out_grad.reshape(rows, width)
    grad_down = product(hidden.T, grad_rows)
    grad_hidden = product(grad_rows, w_down.T)
    unused, gate_back = jax.vjp(gated, gate, upper)
    grad_gate, grad_upper = gate_back(grad_hidden)
    grad_gate = grad_gate.astype(jnp.bfloat16)
    grad_upper = grad_upper.astype(jnp.bfloat16)
    grad_wgate = product(normal_two.T, grad_gate)
    grad_wup = product(normal_two.T, grad_upper)
    grad_normal_two = product(grad_gate, w_gate.T) + product(grad_upper, w_up.T)
    unused_two, norm_back_two = jax.vjp(normed, middle, gain_two_f)
    grad_middle, grad_gain_two = norm_back_two(grad_normal_two)
    grad_middle = grad_middle + grad_rows.astype(jnp.float32)
    ffn_terms = (
        lax.psum_scatter(
            grad_gain_two.astype(jnp.bfloat16), "dp", scatter_dimension=0, tiled=True
        ).astype(jnp.float32),
        lax.psum_scatter(
            grad_wgate.astype(jnp.bfloat16), "dp", scatter_dimension=0, tiled=True
        ).astype(jnp.float32),
        lax.psum_scatter(
            grad_wup.astype(jnp.bfloat16), "dp", scatter_dimension=0, tiled=True
        ).astype(jnp.float32),
        lax.psum_scatter(
            grad_down.astype(jnp.bfloat16), "dp", scatter_dimension=0, tiled=True
        ).astype(jnp.float32),
    )
    ffn_total = (
        lax.psum(ffn_terms[0].astype(jnp.bfloat16), "ctx").astype(jnp.float32),
        lax.psum(ffn_terms[1].astype(jnp.bfloat16), "ctx").astype(jnp.float32),
        lax.psum(ffn_terms[2].astype(jnp.bfloat16), "ctx").astype(jnp.float32),
        lax.psum(ffn_terms[3].astype(jnp.bfloat16), "ctx").astype(jnp.float32),
    )
    grad_branch = grad_middle.astype(jnp.bfloat16)
    grad_woutput = product(mixed_rows.T, grad_branch)
    grad_mixed = product(grad_branch, w_output.T).astype(jnp.bfloat16)
    grad_query, grad_keys_all, grad_values_all = lax.map(
        attend_back, (shaped(query), keys_all, values_all, shaped(grad_mixed), logsum)
    )
    grad_keys, grad_values = (
        lax.psum_scatter(
            grad_keys_all.astype(jnp.bfloat16), "ctx", scatter_dimension=1, tiled=True
        ).astype(jnp.float32),
        lax.psum_scatter(
            grad_values_all.astype(jnp.bfloat16), "ctx", scatter_dimension=1, tiled=True
        ).astype(jnp.float32),
    )
    grad_keys = grad_keys.astype(jnp.bfloat16)
    grad_values = grad_values.astype(jnp.bfloat16)
    grad_query = grad_query.reshape(rows, width)
    grad_keys = grad_keys.reshape(rows, width)
    grad_values = grad_values.reshape(rows, width)
    grad_wquery = product(normal_one.T, grad_query)
    grad_wkey = product(normal_one.T, grad_keys)
    grad_wvalue = product(normal_one.T, grad_values)
    grad_normal_one = (
        product(grad_query, w_query.T)
        + product(grad_keys, w_key.T)
        + product(grad_values, w_value.T)
    )
    unused_one, norm_back_one = jax.vjp(normed, inputs, gain_one_f)
    grad_inputs, grad_gain_one = norm_back_one(grad_normal_one)
    in_grad = (grad_inputs + grad_middle).astype(jnp.bfloat16).reshape(seqs, local, width)
    attn_terms = (
        lax.psum_scatter(
            grad_gain_one.astype(jnp.bfloat16), "dp", scatter_dimension=0, tiled=True
        ).astype(jnp.float32),
        lax.psum_scatter(
            grad_wquery.astype(jnp.bfloat16), "dp", scatter_dimension=0, tiled=True
        ).astype(jnp.float32),
        lax.psum_scatter(
            grad_wkey.astype(jnp.bfloat16), "dp", scatter_dimension=0, tiled=True
        ).astype(jnp.float32),
        lax.psum_scatter(
            grad_wvalue.astype(jnp.bfloat16), "dp", scatter_dimension=0, tiled=True
        ).astype(jnp.float32),
        lax.psum_scatter(
            grad_woutput.astype(jnp.bfloat16), "dp", scatter_dimension=0, tiled=True
        ).astype(jnp.float32),
    )
    attn_total = (
        lax.psum(attn_terms[0].astype(jnp.bfloat16), "ctx").astype(jnp.float32),
        lax.psum(attn_terms[1].astype(jnp.bfloat16), "ctx").astype(jnp.float32),
        lax.psum(attn_terms[2].astype(jnp.bfloat16), "ctx").astype(jnp.float32),
        lax.psum(attn_terms[3].astype(jnp.bfloat16), "ctx").astype(jnp.float32),
        lax.psum(attn_terms[4].astype(jnp.bfloat16), "ctx").astype(jnp.float32),
    )
    return (
        layer_out,
        in_grad,
        attn_total[0],
        attn_total[1],
        attn_total[2],
        attn_total[3],
        attn_total[4],
        ffn_total[0],
        ffn_total[1],
        ffn_total[2],
        ffn_total[3],
    )


def solution(mesh):
    in_specs = (
        P("dp", "ctx", None),
        P("dp", "ctx", None),
        P("dp"),
        P("dp", None),
        P("dp", None),
        P("dp", None),
        P("dp", None),
        P("dp"),
        P("dp", None),
        P("dp", None),
        P("dp", None),
    )
    out_specs = (
        P("dp", "ctx", None),
        P("dp", "ctx", None),
        P("dp"),
        P("dp", None),
        P("dp", None),
        P("dp", None),
        P("dp", None),
        P("dp"),
        P("dp", None),
        P("dp", None),
        P("dp", None),
    )
    return jax.shard_map(
        on_device, mesh=mesh, in_specs=in_specs, out_specs=out_specs, check_vma=False
    )
```

profile of v0, /device:TPU:0, one launch (start us, length us, event | category | flops | bytes accessed | tf_op | source)
XLA Modules:
  0.0 1049.3 jit_solution(17920821551046934564)
XLA Ops:
  13.8 7.7 all-gather.18.cloned.1.call-done
  24.3 9.2 all-gather.14.cloned.1.call-done
  40.8 4.7 all-gather.16.cloned.1.call-done
  47.5 96.6 %all-gather.30.cloned.1.call-done = bf16[4096,768]{1,0:T(8,128)(2,1)} async-done(((bf16[256,768]{1,0:T(8,128)(2,1)}), bf16[4096,768]{1,0:T(8,128)(2,1)}) %all-gather.30.cloned.1.call-update) | async-done | bytes 6291472 | tf_op jit(solution)/shard_map/all_gather | solution.py:115
  144.0 8.7 copy.36
  152.7 22.9 %multiply_reduce_fusion.1 = (f32[12,256]{1,0:T(8,128)S(1)}, f32[12,256,4096]{2,1,0:T(8,128)}) fusion(bf16[256,12,64]{0,2,1:T(8,128)(2,1)S(1)} %bitcast.127, bf16[4096,12,64]{0,2,1:T(8,128)(2,1)} %bitcast.119), kind=kOutput, calls=%fused_computation.6 | convolution fusion | flops 1635775488 | bytes 57028608 | tf_op jit(solution)/shard_map/while/body/eval_jaxpr/qhd,khd->hqk/dot_general | solution.py:24
  175.7 20.5 %fusion = f32[12,256]{1,0:T(8,128)S(1)} fusion(f32[12,256,4096]{2,1,0:T(8,128)} %get-tuple-element.75, f32[12,256]{1,0:T(8,128)S(1)} %get-tuple-element.74), kind=kLoop, calls=%fused_computation.5 | loop fusion | flops 37745664 | bytes 50356224 | tf_op jit(solution)/shard_map/while/body/eval_jaxpr/reduce_sum | solution.py:34
  196.2 43.5 %all-gather.28.cloned.1.call-done = bf16[4096,768]{1,0:T(8,128)(2,1)} async-done(((bf16[256,768]{1,0:T(8,128)(2,1)}), bf16[4096,768]{1,0:T(8,128)(2,1)}) %all-gather.28.cloned.1.call-update) | async-done | bytes 6291472 | tf_op jit(solution)/shard_map/all_gather | solution.py:116
  239.7 8.7 copy.34
  248.4 22.0 %fusion.19 = bf16[12,64,256]{2,1,0:T(8,128)(2,1)S(1)} fusion(bf16[4096,12,64]{0,2,1:T(8,128)(2,1)} %bitcast.121, f32[12,256,4096]{2,1,0:T(8,128)} %get-tuple-element.75, f32[12,256]{1,0:T(8,128)S(1)} %fusion, f32[12,256]{1,0:T(8,128)S(1)} %get-tuple-element.74), kind=kOutput, calls=%fused_computation.45 | convolution fusion | flops 1661140992 | bytes 57040896 | tf_op jit(solution)/shard_map/while/body/eval_jaxpr/hqk,khd->qhd/dot_general | solution.py:36
  272.6 4.6 fusion.57
  278.5 4.2 fusion.58
  282.7 10.7 %all-gather.26.cloned.1.call-done = bf16[2048,768]{1,0:T(8,128)(2,1)} async-done(((bf16[1024,768]{1,0:T(8,128)(2,1)}), bf16[2048,768]{1,0:T(8,128)(2,1)}) %all-gather.26.cloned.1.call-update) | async-done | bytes 3145744 | tf_op jit(solution)/shard_map/all_gather | solution.py:125
  293.3 6.9 multiply_convert_fusion.2
  305.6 35.5 %multiply_reduce_fusion = (f32[12,256]{1,0:T(8,128)}, f32[12,256,4096]{2,1,0:T(8,128)}) fusion(f32[12,256,4096]{2,1,0:T(8,128)} %get-tuple-element.75, f32[12,256]{1,0:T(8,128)S(1)} %log_add_fusion, bf16[256,12,64]{0,2,1:T(8,128)(2,1)S(1)} %bitcast.125, bf16[4096,12,64]{0,2,1:T(8,128)(2,1)} %bitcast.122), kind=kOutput, calls=%fused_computation.1 | convolution fusion | flops 1660941312 | bytes 107372544 | tf_op jit(solution)/shard_map/while/body/eval_jaxpr/qhd,khd->hqk/dot_general | solution.py:43
  341.1 40.2 %multiply_convert_fusion = bf16[12,256,4096]{2,1,0:T(8,128)(2,1)} fusion(f32[12,256,4096]{2,1,0:T(8,128)} %get-tuple-element.80, f32[12,256,4096]{2,1,0:T(8,128)} %get-tuple-element.75, f32[12,256]{1,0:T(8,128)} %get-tuple-element.79, f32[12,256]{1,0:T(8,128)S(1)} %log_add_fusion), kind=kLoop, calls=%fused_computation | loop fusion | flops 62914560 | bytes 125853696 | tf_op jit(solution)/shard_map/while/body/eval_jaxpr/convert_element_type | solution.py:47
  381.3 15.2 %multiply_convert_fusion.1 = bf16[12,64,4096]{2,1,0:T(8,128)(2,1)} fusion(bf16[256,12,64]{0,2,1:T(8,128)(2,1)S(1)} %bitcast.128, bf16[12,256,4096]{2,1,0:T(8,128)(2,1)} %multiply_convert_fusion), kind=kOutput, calls=%fused_computation.12 | convolution fusion | flops 1616904192 | bytes 31850496 | tf_op jit(solution)/shard_map/while/body/eval_jaxpr/hqk,qhd->khd/dot_general | solution.py:62
  396.6 22.0 %fusion.7 = bf16[12,64,4096]{2,1,0:T(8,128)(2,1)} fusion(bf16[256,12,64]{0,2,1:T(8,128)(2,1)S(1)} %bitcast.126, f32[12,256,4096]{2,1,0:T(8,128)} %get-tuple-element.75, f32[12,256]{1,0:T(8,128)S(1)} %log_add_fusion), kind=kOutput, calls=%fused_computation.13 | convolution fusion | flops 1651507200 | bytes 57028608 | tf_op jit(solution)/shard_map/while/body/eval_jaxpr/hqk,qhd->khd/dot_general | solution.py:65
  418.6 14.4 %fusion.18 = bf16[12,64,256]{2,1,0:T(8,128)(2,1)S(1)} fusion(bf16[4096,12,64]{0,2,1:T(8,128)(2,1)} %bitcast.120, bf16[12,256,4096]{2,1,0:T(8,128)(2,1)} %multiply_convert_fusion), kind=kOutput, calls=%fused_computation.44 | convolution fusion | flops 1611005952 | bytes 31850496 | tf_op jit(solution)/shard_map/while/body/eval_jaxpr/hqk,khd->qhd/dot_general | solution.py:52
  436.4 3.9 convolution_convert_fusion.2
  448.3 95.9 %reduce-scatter.10.cloned.1.call-done = bf16[1,256,768]{1,2,0:T(8,128)(2,1)} async-done(((bf16[1,4096,768]{1,2,0:T(8,128)(2,1)}), bf16[1,256,768]{1,2,0:T(8,128)(2,1)}) %reduce-scatter.10.cloned.1.call-update) | async-done | bytes 393232 | tf_op jit(solution)/shard_map/reduce_scatter | solution.py:189
  546.9 148.6 %reduce-scatter.12.cloned.1.call-done = bf16[1,256,768]{1,2,0:T(8,128)(2,1)} async-done(((bf16[1,4096,768]{1,2,0:T(8,128)(2,1)}), bf16[1,256,768]{1,2,0:T(8,128)(2,1)}) %reduce-scatter.12.cloned.1.call-update) | async-done | bytes 393232 | tf_op jit(solution)/shard_map/reduce_scatter | solution.py:192
  698.4 7.6 reduce-scatter.14.cloned.1.call-done
  706.0 12.8 %reduce-scatter.20.cloned.1.call-done = bf16[384,768]{1,0:T(8,128)(2,1)} async-done(((bf16[768,768]{1,0:T(8,128)(2,1)}), bf16[384,768]{1,0:T(8,128)(2,1)}) %reduce-scatter.20.cloned.1.call-update) | async-done | bytes 589840 | tf_op jit(solution)/shard_map/reduce_scatter | solution.py:225
  718.8 14.8 %reduce-scatter.22.cloned.1.call-done = bf16[384,2048]{1,0:T(8,128)(2,1)} async-done(((bf16[768,2048]{1,0:T(8,128)(2,1)}), bf16[384,2048]{1,0:T(8,128)(2,1)}) %reduce-scatter.22.cloned.1.call-update) | async-done | bytes 1572880 | tf_op jit(solution)/shard_map/reduce_scatter | solution.py:166
  733.6 14.9 %reduce-scatter.24.cloned.1.call-done = bf16[384,2048]{1,0:T(8,128)(2,1)} async-done(((bf16[768,2048]{1,0:T(8,128)(2,1)}), bf16[384,2048]{1,0:T(8,128)(2,1)}) %reduce-scatter.24.cloned.1.call-update) | async-done | bytes 1572880 | tf_op jit(solution)/shard_map/reduce_scatter | solution.py:169
  748.4 14.8 %reduce-scatter.26.cloned.1.call-done = bf16[1024,768]{1,0:T(8,128)(2,1)} async-done(((bf16[2048,768]{1,0:T(8,128)(2,1)}), bf16[1024,768]{1,0:T(8,128)(2,1)}) %reduce-scatter.26.cloned.1.call-update) | async-done | bytes 1572880 | tf_op jit(solution)/shard_map/reduce_scatter | solution.py:172
  763.2 12.6 %reduce-scatter.16.cloned.1.call-done = bf16[384,768]{1,0:T(8,128)(2,1)} async-done(((bf16[768,768]{1,0:T(8,128)(2,1)}), bf16[384,768]{1,0:T(8,128)(2,1)}) %reduce-scatter.16.cloned.1.call-update) | async-done | bytes 589840 | tf_op jit(solution)/shard_map/reduce_scatter | solution.py:219
  775.8 12.6 %reduce-scatter.18.cloned.1.call-done = bf16[384,768]{1,0:T(8,128)(2,1)} async-done(((bf16[768,768]{1,0:T(8,128)(2,1)}), bf16[384,768]{1,0:T(8,128)(2,1)}) %reduce-scatter.18.cloned.1.call-update) | async-done | bytes 589840 | tf_op jit(solution)/shard_map/reduce_scatter | solution.py:222
  792.1 3.8 fusion.20
  799.8 43.9 %all-reduce.2 = (bf16[384]{0:T(512)(128)(2,1)S(1)}, bf16[384]{0:T(512)(128)(2,1)S(1)}) all-reduce(bf16[384]{0:T(512)(128)(2,1)S(1)} %dynamic-slice.3, bf16[384]{0:T(512)(128)(2,1)S(1)} %dynamic-slice.5), channel_id=1, replica_groups=mesh['dp'=2,'ctx'=16] {'ctx'}, use_global_device_ids=true, to_apply=%region_11.12 | all-reduce | flops 768 | bytes 3072 | tf_op jit(solution)/shard_map/psum | solution.py:230
  845.9 184.0 %all-reduce.7.cloned.1.call-done = (bf16[384,768]{1,0:T(8,128)(2,1)}, bf16[384,768]{1,0:T(8,128)(2,1)}, bf16[384,768]{1,0:T(8,128)(2,1)}, bf16[384,768]{1,0:T(8,...) async-done(((bf16[384,768]{1,0:T(8,128)(2,1)}, bf16[384,768]{1,0:T(8,128)(2,1)}, bf16[384,768]{1,0:T(8,128)(2,1)}, ...) | async-done | bytes 7077904 | tf_op jit(solution)/shard_map/psum | solution.py:231
  (153 shorter events, 65.7 us)
Async XLA Ops:
  7.2 26.3 %copy-start = (bf16[1,256,768]{2,1,0:T(8,128)(2,1)S(1)}, bf16[1,256,768]{2,1,0:T(8,128)(2,1)}, u32[]{:S(2)}) copy-start(bf16[1,256,768]{2,1,0:T(8,128)(2,1)} %param.11) | copy-start | bytes 1179652
  7.2 14.3 %all-gather.18.cloned.1.call-start = ((), (), s32[]{:S(2)}) async-start(), calls=%async_computation.11 | async-start | bytes 1769472 | tf_op jit(solution)/shard_map/all_gather | solution.py:104
  7.9 25.6 %all-gather.14.cloned.1.call-start = ((), (), s32[]{:S(2)}) async-start(), calls=%async_computation.9 | async-start | bytes 1769472 | tf_op jit(solution)/shard_map/all_gather | solution.py:105
  8.7 36.8 %all-gather.16.cloned.1.call-start = ((), (), s32[]{:S(2)}) async-start(), calls=%async_computation.10 | async-start | bytes 1769472 | tf_op jit(solution)/shard_map/all_gather | solution.py:103
  9.4 134.6 %all-gather.30.cloned.1.call-start = ((), (), s32[]{:S(2)}) async-start(), calls=%async_computation.26 | async-start | bytes 6684672 | tf_op jit(solution)/shard_map/all_gather | solution.py:115
  12.1 33.4 %copy-start.23 = (f32[768]{0:T(1024)}, f32[768]{0:T(1024)S(1)}, u32[]{:S(2)}) copy-start(f32[768]{0:T(1024)S(1)} %reshape.240) | copy-start | bytes 9220
  13.8 31.6 %copy-start.25 = (f32[256]{0:T(256)}, f32[256]{0:T(256)S(1)}, u32[]{:S(2)}) copy-start(f32[256]{0:T(256)S(1)} %fusion.47) | copy-start | bytes 3076
  24.2 215.5 %all-gather.28.cloned.1.call-start = ((), (), s32[]{:S(2)}) async-start(), calls=%async_computation.25 | async-start | bytes 6684672 | tf_op jit(solution)/shard_map/all_gather | solution.py:116
  36.1 234.4 %all-gather.20.cloned.1.call-start = ((), (), s32[]{:S(2)}) async-start(), calls=%async_computation.12 | async-start | bytes 1769472 | tf_op jit(solution)/shard_map/all_gather | solution.py:106
  36.6 235.9 %all-gather.22.cloned.1.call-start = ((), (), s32[]{:S(2)}) async-start(), calls=%async_computation.13 | async-start | bytes 4718592 | tf_op jit(solution)/shard_map/all_gather | solution.py:123
  37.4 241.1 %all-gather.24.cloned.1.call-start = ((), (), s32[]{:S(2)}) async-start(), calls=%async_computation.14 | async-start | bytes 4718592 | tf_op jit(solution)/shard_map/all_gather | solution.py:124
  38.1 255.2 %all-gather.26.cloned.1.call-start = ((), (), s32[]{:S(2)}) async-start(), calls=%async_computation.15 | async-start | bytes 4718592 | tf_op jit(solution)/shard_map/all_gather | solution.py:125
  38.9 505.3 %reduce-scatter.10.cloned.1.call-start = ((), (), s32[]{:S(2)}) async-start(), calls=%async_computation.16 | async-start | bytes 6684672 | tf_op jit(solution)/shard_map/reduce_scatter | solution.py:189
  47.4 105.3 %copy-start.3 = (bf16[256,768]{0,1:T(8,128)(2,1)}, bf16[256,768]{0,1:T(8,128)(2,1)S(1)}, u32[]{:S(2)}) copy-start(bf16[256,768]{0,1:T(8,128)(2,1)S(1)} %copy.35) | copy-start | bytes 1179652
  277.2 16.1 %copy-start.11 = (bf16[1,256,768]{2,1,0:T(8,128)(2,1)S(1)}, bf16[1,256,768]{2,1,0:T(8,128)(2,1)}, u32[]{:S(2)}) copy-start(bf16[1,256,768]{2,1,0:T(8,128)(2,1)} %param.12) | copy-start | bytes 1179652
  293.3 7.0 copy-start.10
  341.1 40.2 %copy-start.4 = (bf16[256,768]{0,1:T(8,128)(2,1)S(1)}, bf16[256,768]{0,1:T(8,128)(2,1)}, u32[]{:S(2)}) copy-start(bf16[256,768]{0,1:T(8,128)(2,1)} %copy-done.3) | copy-start | bytes 1179652
  396.5 299.0 %reduce-scatter.12.cloned.1.call-start = ((), (), s32[]{:S(2)}) async-start(), calls=%async_computation.17 | async-start | bytes 6684672 | tf_op jit(solution)/shard_map/reduce_scatter | solution.py:192
  418.6 14.5 %copy-start.24 = (f32[768]{0:T(1024)S(1)}, f32[768]{0:T(1024)}, u32[]{:S(2)}) copy-start(f32[768]{0:T(1024)} %copy-done.23) | copy-start | bytes 9220
  418.6 14.5 %copy-start.26 = (f32[256]{0:T(256)S(1)}, f32[256]{0:T(256)}, u32[]{:S(2)}) copy-start(f32[256]{0:T(256)} %copy-done.25) | copy-start | bytes 3076
  418.6 287.4 %reduce-scatter.14.cloned.1.call-start = ((), (), s32[]{:S(2)}) async-start(), calls=%async_computation.18 | async-start | bytes 1769472 | tf_op jit(solution)/shard_map/reduce_scatter | solution.py:216
  434.7 284.0 %reduce-scatter.20.cloned.1.call-start = ((), (), s32[]{:S(2)}) async-start(), calls=%async_computation.21 | async-start | bytes 1769472 | tf_op jit(solution)/shard_map/reduce_scatter | solution.py:225
  436.3 297.2 %reduce-scatter.22.cloned.1.call-start = ((), (), s32[]{:S(2)}) async-start(), calls=%async_computation.22 | async-start | bytes 4718592 | tf_op jit(solution)/shard_map/reduce_scatter | solution.py:166
  440.3 308.1 %reduce-scatter.24.cloned.1.call-start = ((), (), s32[]{:S(2)}) async-start(), calls=%async_computation.23 | async-start | bytes 4718592 | tf_op jit(solution)/shard_map/reduce_scatter | solution.py:169
  444.2 318.9 %reduce-scatter.26.cloned.1.call-start = ((), (), s32[]{:S(2)}) async-start(), calls=%async_computation.24 | async-start | bytes 4718592 | tf_op jit(solution)/shard_map/reduce_scatter | solution.py:172
  448.3 327.5 %reduce-scatter.16.cloned.1.call-start = ((), (), s32[]{:S(2)}) async-start(), calls=%async_computation.19 | async-start | bytes 1769472 | tf_op jit(solution)/shard_map/reduce_scatter | solution.py:219
  546.8 241.5 %reduce-scatter.18.cloned.1.call-start = ((), (), s32[]{:S(2)}) async-start(), calls=%async_computation.20 | async-start | bytes 1769472 | tf_op jit(solution)/shard_map/reduce_scatter | solution.py:222
  698.1 331.8 %all-reduce.7.cloned.1.call-start = ((), (), s32[]{:S(2)}) async-start(), calls=%async_computation.27 | async-start | bytes 14155776 | tf_op jit(solution)/shard_map/psum | solution.py:231
  795.9 49.0 %copy-start.28 = (f32[256]{0:T(256)S(1)}, f32[256]{0:T(256)}, u32[]{:S(2)}) copy-start(f32[256]{0:T(256)} %copy-done.27) | copy-start | bytes 3076
  1029.9 4.5 copy-start.22
  1029.9 5.6 copy-start.21
  1029.9 6.7 copy-start.17
  (19 other events, 49.2 us)
Sparse Core Ops, SparseCore 0:
  9.6 11.9 all-gather.17
  23.1 10.3 all-gather.13
  35.0 10.3 all-gather.15
  48.7 95.2 all-gather.29
  147.2 92.4 all-gather.27
  241.1 7.4 all-gather.19
  250.2 13.2 all-gather.21
  265.0 13.3 all-gather.23
  280.0 13.2 all-gather.25
  396.6 147.5 reduce-scatter.9
  549.4 146.0 reduce-scatter.11
  698.1 7.7 reduce-scatter.13
  708.9 9.8 reduce-scatter.19
  721.4 12.0 reduce-scatter.21
  736.3 12.0 reduce-scatter.23
  751.1 12.0 reduce-scatter.25
  765.9 9.8 reduce-scatter.15
  778.5 9.8 reduce-scatter.17
  795.9 233.8 all-reduce.6
where the time goes:
time: 1060 us; the launch traced here: 1050 us
  waiting for transfers between devices  697 us (66%)
  matrix products  184 us (17%)
  other arithmetic  77.1 us (7%)
  blocking collectives  50.1 us (5%)
  local copies, waits for them, and re-layouts  24.6 us (2%)
  between operations  15.3 us (1%)
    psum x1, waiting for transfers between devices, on_device(): lax.psum(attn_terms[1].astype(jnp.bfloat16), 'ctx').astype(jnp.float32)  184 us
    reduce_scatter x1, waiting for transfers between devices, on_device(): lax.psum_scatter(grad_values_all.astype(jnp.bfloat16), 'ctx', scatter_dim...  149 us
    all_gather x1, waiting for transfers between devices, on_device(): lax.all_gather(shaped(keys), 'ctx', axis=1, tiled=True)  96.6 us
    reduce_scatter x1, waiting for transfers between devices, on_device(): lax.psum_scatter(grad_keys_all.astype(jnp.bfloat16), 'ctx', scatter_dimen...  95.9 us
    dot_general x21, matrix products, product(): return jnp.dot(left, right, preferred_element_type=jnp.float32)  52.2 us
    psum x1, blocking collectives, on_device(): lax.psum(attn_terms[0].astype(jnp.bfloat16), 'ctx').astype(jnp.float32)  43.9 us
    all_gather x1, waiting for transfers between devices, on_device(): lax.all_gather(shaped(values), 'ctx', axis=1, tiled=True)  43.5 us
    convert_element_type x1, other arithmetic, back_core(): grad_score = (probs * (grad_prob - delta[..., None])).astype(jnp.bfloat16)  40.2 us
  transfers between devices with their start and end apart: 19, of which 17 were waited for; matrix products, arithmetic and copies ran while one was open for 16% of the time, Pallas kernels for 0%

commit v1 on v0

--- a/solution.py
+++ b/solution.py
@@ -6,6 +6,18 @@
 HEADS = 12
 HEAD_DIM = 64
 EPS = 1e-06
+
+
+def collect(x, axis, dim):
+    ways, here = (lax.axis_size(axis), lax.axis_index(axis))
+    grown, reach = (x, 1)
+    while reach < ways:
+        theirs = lax.ppermute(grown, axis, [(d, d ^ reach) for d in range(ways)])
+        mine_first = jnp.concatenate([grown, theirs], axis=dim)
+        theirs_first = jnp.concatenate([theirs, grown], axis=dim)
+        grown = jnp.where(here & reach == 0, mine_first, theirs_first)
+        reach = 2 * reach
+    return grown
 
 
 def normed(rows, gain):
@@ -113,7 +125,7 @@
     values = product(normal_one, w_value).astype(jnp.bfloat16)
     keys_all, values_all = (
         lax.all_gather(shaped(keys), "ctx", axis=1, tiled=True),
-        lax.all_gather(shaped(values), "ctx", axis=1, tiled=True),
+        collect(shaped(values), "ctx", 1),
     )
     mixed, logsum = lax.map(attend, (shaped(query), keys_all, values_all))
     mixed_rows = mixed.reshape(rows, width)

time: 1060 us -> 1140 us (1.075)
  waiting for transfers between devices: 697 us -> 764 us
  other arithmetic: 77.1 us -> 92.6 us
    ppermute x0 -> x4, waiting for transfers between devices: none -> 228 us  [collect(): theirs = lax.ppermute(grown, axis, [(d, d ^ reach) for d in range(ways)])]
    all_gather x1, waiting for transfers between devices: 96.6 us -> 0.01 us  [on_device(): lax.all_gather(shaped(keys), 'ctx', axis=1, tiled=True)]
    all_gather x1 -> x0, waiting for transfers between devices: 43.5 us -> none  [on_device(): lax.all_gather(shaped(values), 'ctx', axis=1, tiled=True)]
    select_n x0 -> x7, other arithmetic: none -> 13.4 us  [collect(): grown = jnp.where(here & reach == 0, mine_first, theirs_first)]
  transfers between devices with their start and end apart: 19 -> 22, of which waited for: 17 -> 16; matrix products, arithmetic and copies ran while one was open for 16% -> 16% of each run, Pallas kernels for 0% -> 0%
where the time goes in v1:
time: 1140 us
  waiting for transfers between devices  764 us (67%)
  matrix products  183 us (16%)
  other arithmetic  92.6 us (8%)
  blocking collectives  50.1 us (4%)
  local copies, waits for them, and re-layouts  27 us (2%)
  between operations  15.7 us (1%)
    ppermute x4, waiting for transfers between devices, collect(): theirs = lax.ppermute(grown, axis, [(d, d ^ reach) for d in range(ways)])  228 us
    psum x1, waiting for transfers between devices, on_device(): lax.psum(attn_terms[1].astype(jnp.bfloat16), 'ctx').astype(jnp.float32)  184 us
    reduce_scatter x1, waiting for transfers between devices, on_device(): lax.psum_scatter(grad_values_all.astype(jnp.bfloat16), 'ctx', scatter_dim...  148 us
    reduce_scatter x1, waiting for transfers between devices, on_device(): lax.psum_scatter(grad_keys_all.astype(jnp.bfloat16), 'ctx', scatter_dimen...  94.1 us
    dot_general x21, matrix products, product(): return jnp.dot(left, right, preferred_element_type=jnp.float32)  50.5 us
    psum x1, blocking collectives, on_device(): lax.psum(attn_terms[0].astype(jnp.bfloat16), 'ctx').astype(jnp.float32)  43.9 us
    convert_element_type x1, other arithmetic, back_core(): grad_score = (probs * (grad_prob - delta[..., None])).astype(jnp.bfloat16)  40.1 us
    dot_general x1, matrix products, back_core(): jnp.einsum('qhd,khd->hqk', heads_of(grad_mix), heads_of(values), preferre...  39.9 us
  transfers between devices with their start and end apart: 22, of which 16 were waited for; matrix products, arithmetic and copies ran while one was open for 16% of the time, Pallas kernels for 0%

profile of v1, /device:TPU:0, one launch (start us, length us, event | category | flops | bytes accessed | tf_op | source)
XLA Modules:
  0.0 1138.8 jit_solution(1294863059677519377)
XLA Ops:
  13.3 8.2 all-gather.16.cloned.1.call-done
  25.4 8.1 all-gather.12.cloned.1.call-done
  37.1 9.6 collective-permute-done
  49.1 19.7 %collective-permute-done.1 = bf16[1,512,768]{2,1,0:T(8,128)(2,1)S(1)} collective-permute-done((bf16[1,512,768]{2,1,0:T(8,128)(2,1)S(1)}, bf16[1,512,768]{2,1,0:T(8,128)(2,1)S(1)}, u32[]{:S(2)}, u32[]{:S(2)}) %collective-permute-start.1) | collective-permute-done | bytes 786464 | tf_op jit(solution)/shard_map/ppermute | solution.py:15
  73.2 52.8 %collective-permute-done.2 = bf16[1,1024,768]{2,1,0:T(8,128)(2,1)S(1)} collective-permute-done((bf16[1,1024,768]{2,1,0:T(8,128)(2,1)}, bf16[1,1024,768]{2,1,0:T(8,128)(2,1)S(1)}, u32[]{:S(2)}, u32[]{:S(2)}) %collective-permute-start.2) | collective-permute-done | bytes 1572896 | tf_op jit(solution)/shard_map/ppermute | solution.py:15
  143.4 4.2 maximum_select_fusion.1
  147.6 145.9 %collective-permute-done.3 = bf16[1,2048,768]{2,1,0:T(8,128)(2,1)} collective-permute-done((bf16[1,2048,768]{2,1,0:T(8,128)(2,1)}, bf16[1,2048,768]{2,1,0:T(8,128)(2,1)}, u32[]{:S(2)}, u32[]{:S(2)}) %collective-permute-start.3) | collective-permute-done | bytes 3145760 | tf_op jit(solution)/shard_map/ppermute | solution.py:15
  293.5 4.6 copy.50
  298.1 8.7 copy.52
  306.8 21.4 %multiply_reduce_fusion.1 = (f32[12,256]{1,0:T(8,128)S(1)}, f32[12,256,4096]{2,1,0:T(8,128)}) fusion(bf16[256,12,64]{0,2,1:T(8,128)(2,1)} %bitcast.136, bf16[4096,12,64]{0,2,1:T(8,128)(2,1)} %bitcast.127), kind=kOutput, calls=%fused_computation.6 | convolution fusion | flops 1635775488 | bytes 57028608 | tf_op jit(solution)/shard_map/while/body/eval_jaxpr/qhd,khd->hqk/dot_general | solution.py:36
  328.2 20.7 %fusion = f32[12,256]{1,0:T(8,128)S(1)} fusion(f32[12,256,4096]{2,1,0:T(8,128)} %get-tuple-element.75, f32[12,256]{1,0:T(8,128)S(1)} %get-tuple-element.74), kind=kLoop, calls=%fused_computation.5 | loop fusion | flops 37745664 | bytes 50356224 | tf_op jit(solution)/shard_map/while/body/eval_jaxpr/reduce_sum | solution.py:46
  349.5 19.6 %fusion.20 = bf16[12,64,256]{2,1,0:T(8,128)(2,1)} fusion(f32[12,256,4096]{2,1,0:T(8,128)} %get-tuple-element.75, f32[12,256]{1,0:T(8,128)S(1)} %fusion, f32[12,256]{1,0:T(8,128)S(1)} %get-tuple-element.74, bf16[2048,12,64]{0,2,1:T(8,128)(2,1)S(1)} %bitcast.132, bf16[2048,12,64]{0,2,1:T(8,128)(2,1)S(1)} %maximum_select_fusion.1, pred[]{:T(512)S(6)} %eq.12), kind=kOutput, calls=%fused_computation.52 | convolution fusion | flops 1689452544 | bytes 57040896 | tf_op jit(solution)/shard_map/while/body/eval_jaxpr/hqk,khd->qhd/dot_general | solution.py:48
  372.6 4.2 fusion.61
  376.8 4.3 fusion.62
  381.1 6.7 multiply_convert_fusion.2
  392.7 39.9 %multiply_reduce_fusion = (f32[12,256]{1,0:T(8,128)S(1)}, f32[12,256,4096]{2,1,0:T(8,128)}) fusion(f32[12,256,4096]{2,1,0:T(8,128)} %get-tuple-element.75, f32[12,256]{1,0:T(8,128)S(1)} %log_add_fusion, bf16[256,12,64]{0,2,1:T(8,128)(2,1)S(1)} %bitcast.140, bf16[2048,12,64]{0,2,1:T(8,128)(2,1)} %bitcast.131, bf16[2048,12,64]{0,2,1:T(8,128)(2,1)} %copy-done.2, ...), kind=kOutput, calls=%fused_computation.1 | convolution fusion | flops 1689252864 | bytes 107372544 | tf_op jit(solution)/shard_map/while/body/eval_jaxpr/qhd,khd->hqk/dot_general | solution.py:55
  432.5 40.1 %multiply_convert_fusion = bf16[12,256,4096]{2,1,0:T(8,128)(2,1)} fusion(f32[12,256,4096]{2,1,0:T(8,128)} %get-tuple-element.80, f32[12,256,4096]{2,1,0:T(8,128)} %get-tuple-element.75, f32[12,256]{1,0:T(8,128)S(1)} %get-tuple-element.79, f32[12,256]{1,0:T(8,128)S(1)} %log_add_fusion), kind=kLoop, calls=%fused_computation | loop fusion | flops 62914560 | bytes 125853696 | tf_op jit(solution)/shard_map/while/body/eval_jaxpr/convert_element_type | solution.py:59
  472.6 15.2 %multiply_convert_fusion.1 = bf16[12,64,4096]{2,1,0:T(8,128)(2,1)} fusion(bf16[256,12,64]{0,2,1:T(8,128)(2,1)S(1)} %bitcast.137, bf16[12,256,4096]{2,1,0:T(8,128)(2,1)} %multiply_convert_fusion), kind=kOutput, calls=%fused_computation.12 | convolution fusion | flops 1616904192 | bytes 31850496 | tf_op jit(solution)/shard_map/while/body/eval_jaxpr/hqk,qhd->khd/dot_general | solution.py:74
  487.9 22.1 %fusion.7 = bf16[12,64,4096]{2,1,0:T(8,128)(2,1)} fusion(bf16[256,12,64]{0,2,1:T(8,128)(2,1)S(1)} %bitcast.141, f32[12,256,4096]{2,1,0:T(8,128)} %get-tuple-element.75, f32[12,256]{1,0:T(8,128)S(1)} %log_add_fusion), kind=kOutput, calls=%fused_computation.13 | convolution fusion | flops 1651507200 | bytes 57028608 | tf_op jit(solution)/shard_map/while/body/eval_jaxpr/hqk,qhd->khd/dot_general | solution.py:77
  510.1 14.4 %fusion.19 = bf16[12,64,256]{2,1,0:T(8,128)(2,1)S(1)} fusion(bf16[4096,12,64]{0,2,1:T(8,128)(2,1)} %bitcast.128, bf16[12,256,4096]{2,1,0:T(8,128)(2,1)} %multiply_convert_fusion), kind=kOutput, calls=%fused_computation.51 | convolution fusion | flops 1611005952 | bytes 31850496 | tf_op jit(solution)/shard_map/while/body/eval_jaxpr/hqk,khd->qhd/dot_general | solution.py:64
  527.8 3.9 convolution_convert_fusion.2
  539.8 94.1 %reduce-scatter.10.cloned.1.call-done = bf16[1,256,768]{1,2,0:T(8,128)(2,1)} async-done(((bf16[1,4096,768]{1,2,0:T(8,128)(2,1)}), bf16[1,256,768]{1,2,0:T(8,128)(2,1)}) %reduce-scatter.10.cloned.1.call-update) | async-done | bytes 393232 | tf_op jit(solution)/shard_map/reduce_scatter | solution.py:201
  636.6 148.3 %reduce-scatter.12.cloned.1.call-done = bf16[1,256,768]{1,2,0:T(8,128)(2,1)} async-done(((bf16[1,4096,768]{1,2,0:T(8,128)(2,1)}), bf16[1,256,768]{1,2,0:T(8,128)(2,1)}) %reduce-scatter.12.cloned.1.call-update) | async-done | bytes 393232 | tf_op jit(solution)/shard_map/reduce_scatter | solution.py:204
  787.8 7.7 reduce-scatter.14.cloned.1.call-done
  795.5 12.6 %reduce-scatter.20.cloned.1.call-done = bf16[384,768]{1,0:T(8,128)(2,1)} async-done(((bf16[768,768]{1,0:T(8,128)(2,1)}), bf16[384,768]{1,0:T(8,128)(2,1)}) %reduce-scatter.20.cloned.1.call-update) | async-done | bytes 589840 | tf_op jit(solution)/shard_map/reduce_scatter | solution.py:237
  808.1 14.9 %reduce-scatter.22.cloned.1.call-done = bf16[384,2048]{1,0:T(8,128)(2,1)} async-done(((bf16[768,2048]{1,0:T(8,128)(2,1)}), bf16[384,2048]{1,0:T(8,128)(2,1)}) %reduce-scatter.22.cloned.1.call-update) | async-done | bytes 1572880 | tf_op jit(solution)/shard_map/reduce_scatter | solution.py:178
  823.1 14.8 %reduce-scatter.24.cloned.1.call-done = bf16[384,2048]{1,0:T(8,128)(2,1)} async-done(((bf16[768,2048]{1,0:T(8,128)(2,1)}), bf16[384,2048]{1,0:T(8,128)(2,1)}) %reduce-scatter.24.cloned.1.call-update) | async-done | bytes 1572880 | tf_op jit(solution)/shard_map/reduce_scatter | solution.py:181
  837.9 14.8 %reduce-scatter.26.cloned.1.call-done = bf16[1024,768]{1,0:T(8,128)(2,1)} async-done(((bf16[2048,768]{1,0:T(8,128)(2,1)}), bf16[1024,768]{1,0:T(8,128)(2,1)}) %reduce-scatter.26.cloned.1.call-update) | async-done | bytes 1572880 | tf_op jit(solution)/shard_map/reduce_scatter | solution.py:184
  852.7 12.6 %reduce-scatter.16.cloned.1.call-done = bf16[384,768]{1,0:T(8,128)(2,1)} async-done(((bf16[768,768]{1,0:T(8,128)(2,1)}), bf16[384,768]{1,0:T(8,128)(2,1)}) %reduce-scatter.16.cloned.1.call-update) | async-done | bytes 589840 | tf_op jit(solution)/shard_map/reduce_scatter | solution.py:231
  865.3 12.6 %reduce-scatter.18.cloned.1.call-done = bf16[384,768]{1,0:T(8,128)(2,1)} async-done(((bf16[768,768]{1,0:T(8,128)(2,1)}), bf16[384,768]{1,0:T(8,128)(2,1)}) %reduce-scatter.18.cloned.1.call-update) | async-done | bytes 589840 | tf_op jit(solution)/shard_map/reduce_scatter | solution.py:234
  889.2 43.9 %all-reduce.2 = (bf16[384]{0:T(512)(128)(2,1)S(1)}, bf16[384]{0:T(512)(128)(2,1)S(1)}) all-reduce(bf16[384]{0:T(512)(128)(2,1)S(1)} %dynamic-slice.3, bf16[384]{0:T(512)(128)(2,1)S(1)} %dynamic-slice.5), channel_id=1, replica_groups=mesh['dp'=2,'ctx'=16] {'ctx'}, use_global_device_ids=true, to_apply=%region_11.12 | all-reduce | flops 768 | bytes 3072 | tf_op jit(solution)/shard_map/psum | solution.py:242
  935.3 183.8 %all-reduce.7.cloned.1.call-done = (bf16[384,768]{1,0:T(8,128)(2,1)}, bf16[384,768]{1,0:T(8,128)(2,1)}, bf16[384,768]{1,0:T(8,128)(2,1)}, bf16[384,768]{1,0:T(8,...) async-done(((bf16[384,768]{1,0:T(8,128)(2,1)}, bf16[384,768]{1,0:T(8,128)(2,1)}, bf16[384,768]{1,0:T(8,128)(2,1)}, ...) | async-done | bytes 7077904 | tf_op jit(solution)/shard_map/psum | solution.py:243
  (184 shorter events, 88.8 us)
Async XLA Ops:
  7.2 14.3 %all-gather.16.cloned.1.call-start = ((), (), s32[]{:S(2)}) async-start(), calls=%async_computation.11 | async-start | bytes 1769472 | tf_op jit(solution)/shard_map/all_gather | solution.py:116
  7.9 25.6 %copy-start = (bf16[1,256,768]{2,1,0:T(8,128)(2,1)S(1)}, bf16[1,256,768]{2,1,0:T(8,128)(2,1)}, u32[]{:S(2)}) copy-start(bf16[1,256,768]{2,1,0:T(8,128)(2,1)} %param.11) | copy-start | bytes 1179652
  7.9 25.6 %all-gather.12.cloned.1.call-start = ((), (), s32[]{:S(2)}) async-start(), calls=%async_computation.9 | async-start | bytes 1769472 | tf_op jit(solution)/shard_map/all_gather | solution.py:117
  8.7 123.1 %all-gather.14.cloned.1.call-start = ((), (), s32[]{:S(2)}) async-start(), calls=%async_computation.10 | async-start | bytes 1769472 | tf_op jit(solution)/shard_map/all_gather | solution.py:115
  9.4 288.7 %all-gather.26.cloned.1.call-start = ((), (), s32[]{:S(2)}) async-start(), calls=%async_computation.25 | async-start | bytes 6684672 | tf_op jit(solution)/shard_map/all_gather | solution.py:127
  12.1 119.7 %copy-start.29 = (f32[768]{0:T(1024)}, f32[768]{0:T(1024)S(1)}, u32[]{:S(2)}) copy-start(f32[768]{0:T(1024)S(1)} %reshape.582) | copy-start | bytes 9220
  13.3 118.6 %copy-start.33 = (f32[256]{0:T(256)}, f32[256]{0:T(256)S(1)}, u32[]{:S(2)}) copy-start(f32[256]{0:T(256)S(1)} %fusion.49) | copy-start | bytes 3076
  24.2 344.9 %all-gather.18.cloned.1.call-start = ((), (), s32[]{:S(2)}) async-start(), calls=%async_computation.12 | async-start | bytes 1769472 | tf_op jit(solution)/shard_map/all_gather | solution.py:118
  24.8 347.8 %all-gather.20.cloned.1.call-start = ((), (), s32[]{:S(2)}) async-start(), calls=%async_computation.13 | async-start | bytes 4718592 | tf_op jit(solution)/shard_map/all_gather | solution.py:135
  25.4 351.5 %all-gather.22.cloned.1.call-start = ((), (), s32[]{:S(2)}) async-start(), calls=%async_computation.14 | async-start | bytes 4718592 | tf_op jit(solution)/shard_map/all_gather | solution.py:136
  35.3 33.5 %copy-start.13 = (bf16[256,768]{1,0:T(8,128)(2,1)}, bf16[256,768]{1,0:T(8,128)(2,1)S(1)}, u32[]{:S(2)}) copy-start(bf16[256,768]{1,0:T(8,128)(2,1)S(1)} %convolution_convert_fusion.10) | copy-start | bytes 1179652
  35.3 11.4 collective-permute-start
  46.7 22.1 %copy-start.11 = (bf16[1,256,768]{2,1,0:T(8,128)(2,1)}, bf16[1,256,768]{2,1,0:T(8,128)(2,1)S(1)}, u32[]{:S(2)}) copy-start(bf16[1,256,768]{2,1,0:T(8,128)(2,1)S(1)} %collective-permute-done) | copy-start | bytes 1179652
  47.0 21.8 %collective-permute-start.1 = (bf16[1,512,768]{2,1,0:T(8,128)(2,1)S(1)}, bf16[1,512,768]{2,1,0:T(8,128)(2,1)S(1)}, u32[]{:S(2)}, u32[]{:S(2)}) collective-permute-start(bf16[1,512,768]{2,1,0:T(8,128)(2,1)S(1)} %maximum_select_fusion.9), channel_id=1, source_target_pairs={{0,2},{1,3},{2,0},{3,1},{4,6},{5,7},{6,4},{7,5},{8,10},{9,11},{10,... | collective-permute-start | bytes 2359304 | tf_op jit(solution)/shard_map/ppermute | solution.py:15
  70.6 55.4 %collective-permute-start.2 = (bf16[1,1024,768]{2,1,0:T(8,128)(2,1)}, bf16[1,1024,768]{2,1,0:T(8,128)(2,1)S(1)}, u32[]{:S(2)}, u32[]{:S(2)}) collective-permute-start(bf16[1,1024,768]{2,1,0:T(8,128)(2,1)} %maximum_select_fusion.4), channel_id=1, source_target_pairs={{0,4},{1,5},{2,6},{3,7},{4,0},{5,1},{6,2},{7,3},{8,12},{9,13},{10,... | collective-permute-start | bytes 4718600 | tf_op jit(solution)/shard_map/ppermute | solution.py:15
  72.4 308.7 %all-gather.24.cloned.1.call-start = ((), (), s32[]{:S(2)}) async-start(), calls=%async_computation.15 | async-start | bytes 4718592 | tf_op jit(solution)/shard_map/all_gather | solution.py:137
  73.1 55.3 %copy-start.37 = (bf16[384]{0:T(512)(128)(2,1)S(1)}, bf16[384]{0:T(512)(128)(2,1)}, u32[]{:S(2)}) copy-start(bf16[384]{0:T(512)(128)(2,1)} %param.18) | copy-start | bytes 2308
  73.2 57.7 %copy-start.14 = (bf16[256,768]{1,0:T(8,128)(2,1)S(1)}, bf16[256,768]{1,0:T(8,128)(2,1)}, u32[]{:S(2)}) copy-start(bf16[256,768]{1,0:T(8,128)(2,1)} %copy-done.13) | copy-start | bytes 1179652
  128.1 165.4 %collective-permute-start.3 = (bf16[1,2048,768]{2,1,0:T(8,128)(2,1)}, bf16[1,2048,768]{2,1,0:T(8,128)(2,1)}, u32[]{:S(2)}, u32[]{:S(2)}) collective-permute-start(bf16[1,2048,768]{2,1,0:T(8,128)(2,1)} %maximum_select_fusion.2), channel_id=1, source_target_pairs={{0,8},{1,9},{2,10},{3,11},{4,12},{5,13},{6,14},{7,15},{8,0},{9,1},... | collective-permute-start | bytes 9437192 | tf_op jit(solution)/shard_map/ppermute | solution.py:15
  128.4 505.5 %reduce-scatter.10.cloned.1.call-start = ((), (), s32[]{:S(2)}) async-start(), calls=%async_computation.16 | async-start | bytes 6684672 | tf_op jit(solution)/shard_map/reduce_scatter | solution.py:201
  147.6 201.3 %copy-start.2 = (bf16[2048,12,64]{0,2,1:T(8,128)(2,1)}, bf16[2048,12,64]{0,2,1:T(8,128)(2,1)S(1)}, u32[]{:S(2)}) copy-start(bf16[2048,12,64]{0,2,1:T(8,128)(2,1)S(1)} %maximum_select_fusion.1) | copy-start | bytes 9437188
  432.5 40.1 %copy-start.5 = (bf16[256,768]{0,1:T(8,128)(2,1)S(1)}, bf16[256,768]{0,1:T(8,128)(2,1)}, u32[]{:S(2)}) copy-start(bf16[256,768]{0,1:T(8,128)(2,1)} %copy.51) | copy-start | bytes 1179652
  487.9 296.9 %reduce-scatter.12.cloned.1.call-start = ((), (), s32[]{:S(2)}) async-start(), calls=%async_computation.17 | async-start | bytes 6684672 | tf_op jit(solution)/shard_map/reduce_scatter | solution.py:204
  510.1 285.4 %reduce-scatter.14.cloned.1.call-start = ((), (), s32[]{:S(2)}) async-start(), calls=%async_computation.18 | async-start | bytes 1769472 | tf_op jit(solution)/shard_map/reduce_scatter | solution.py:228
  526.2 281.9 %reduce-scatter.20.cloned.1.call-start = ((), (), s32[]{:S(2)}) async-start(), calls=%async_computation.21 | async-start | bytes 1769472 | tf_op jit(solution)/shard_map/reduce_scatter | solution.py:237
  527.8 295.3 %reduce-scatter.22.cloned.1.call-start = ((), (), s32[]{:S(2)}) async-start(), calls=%async_computation.22 | async-start | bytes 4718592 | tf_op jit(solution)/shard_map/reduce_scatter | solution.py:178
  531.8 306.2 %reduce-scatter.24.cloned.1.call-start = ((), (), s32[]{:S(2)}) async-start(), calls=%async_computation.23 | async-start | bytes 4718592 | tf_op jit(solution)/shard_map/reduce_scatter | solution.py:181
  535.7 317.0 %reduce-scatter.26.cloned.1.call-start = ((), (), s32[]{:S(2)}) async-start(), calls=%async_computation.24 | async-start | bytes 4718592 | tf_op jit(solution)/shard_map/reduce_scatter | solution.py:184
  539.7 325.6 %reduce-scatter.16.cloned.1.call-start = ((), (), s32[]{:S(2)}) async-start(), calls=%async_computation.19 | async-start | bytes 1769472 | tf_op jit(solution)/shard_map/reduce_scatter | solution.py:231
  636.5 241.3 %reduce-scatter.18.cloned.1.call-start = ((), (), s32[]{:S(2)}) async-start(), calls=%async_computation.20 | async-start | bytes 1769472 | tf_op jit(solution)/shard_map/reduce_scatter | solution.py:234
  787.5 331.6 %all-reduce.7.cloned.1.call-start = ((), (), s32[]{:S(2)}) async-start(), calls=%async_computation.26 | async-start | bytes 14155776 | tf_op jit(solution)/shard_map/psum | solution.py:243
  885.4 48.9 %copy-start.36 = (f32[256]{0:T(256)S(1)}, f32[256]{0:T(256)}, u32[]{:S(2)}) copy-start(f32[256]{0:T(256)} %copy-done.35) | copy-start | bytes 3076
  (29 other events, 154.2 us)
Sparse Core Ops, SparseCore 0:
  9.6 11.9 all-gather.15
  23.1 10.3 all-gather.11
  35.0 10.3 all-gather.13
  48.7 192.2 all-gather.25
  242.4 8.7 all-gather.17
  252.6 13.2 all-gather.19
  267.5 13.2 all-gather.21
  282.4 13.2 all-gather.23
  488.0 145.8 reduce-scatter.9
  639.0 145.8 reduce-scatter.11
  787.7 7.7 reduce-scatter.13
  798.3 9.8 reduce-scatter.19
  811.0 12.0 reduce-scatter.21
  825.9 12.0 reduce-scatter.23
  840.6 12.0 reduce-scatter.25
  855.5 9.8 reduce-scatter.15
  868.0 9.8 reduce-scatter.17
  885.3 233.7 all-reduce.6
